TPU v7x, 32 devices: a whole 2x2x4 slice. The times are simulated.
32 devices in a mesh: groups: 2 (over x), seq: 16 (over z, y, core).
Axes of the slice: x: 2, y: 2, z: 4, core: 2. Of those that a mesh axis runs over, the one named last changes fastest.
Arguments:
- queries: bfloat16 [8192, 2048], P(('groups', 'seq')), parts along dimension 0, may hold values from -14 to 14
- ctx_keys: bfloat16 [8192, 512], P(('groups', 'seq')), parts along dimension 0, may hold values from -11.5 to 11.5
- ctx_values: bfloat16 [8192, 512], P(('groups', 'seq')), parts along dimension 0, may hold values from -5 to 5
- store_keys: bfloat16 [512, 128, 512], P(('groups', 'seq')), parts along dimension 0, may hold values from -11.5 to 11.5
- store_values: bfloat16 [512, 128, 512], P(('groups', 'seq')), parts along dimension 0, may hold values from -5 to 5
- block_ids: int32 [32, 32], P(('groups', 'seq')), parts along dimension 0, may hold values from 0 to 255, as said below
- block_slot: int32 [512], P('groups'), parts along dimension 0, may hold values from 0 to 255, as said below
- gate_logit: float32 [16], replicated, may hold values from -2 to 2
Outputs:
- mixed: bfloat16 [8192, 2048], P(('groups', 'seq')), parts along dimension 0
There are 2 independent parts, one for each index of `groups`. A program takes and returns all parts, laid end to end along the dimension named above; an argument that names none is the same for every part. Nothing has to cross between parts.
Inputs may be any that keep to these rules, and one draw needn't show every extreme that they name: block_slot is a permutation of 0 to 255; memory block b lies on seq index block_slot[b] // 16 at local position block_slot[b] % 16. `block_ids`: the 32 ids of one row are distinct; at most 2 of them lie on any one seq index, and in every draw some seq index holds exactly 2 blocks of every row.
All inputs are finite; a program needn't handle non-finite values.
Results may differ from a plain program's by a relative error of at most 0.0052.
Values may be sent and summed in bfloat16 or wider, within the bound.
A program may use at most 192 MiB of HBM per device.

v0:
```python
import math

import jax
import jax.numpy as jnp
from jax import lax
from jax.sharding import PartitionSpec as P

H = 16
KVH = 4
HD = 128
QBLK = 256
MROWS = 128
TOPM = 32
CAP = 2


masked_score = -1e30
key_block = 1024


def fresh_state(row_count, kv_heads):
    group = H // KVH
    return (
        jnp.full((kv_heads, group, row_count), masked_score, jnp.float32),
        jnp.zeros((kv_heads, group, row_count), jnp.float32),
        jnp.zeros((kv_heads, group, row_count, HD), jnp.float32),
    )


def split_heads(query_part):
    group = H // KVH
    kv_heads = query_part.shape[1] // (group * HD)
    return query_part.reshape(query_part.shape[0], kv_heads, group, HD)


def block_update(state, query_heads, key_rows, value_rows, allowed):
    row_max, row_sum, weighted = state
    kv_heads = query_heads.shape[1]
    scores = jnp.einsum(
        "rhgd,khd->hgrk",
        query_heads,
        key_rows.reshape(-1, kv_heads, HD),
        preferred_element_type=jnp.float32,
    ) * HD ** (-0.5)
    if allowed is not None:
        scores = jnp.where(allowed, scores, masked_score)
    new_max = jnp.maximum(row_max, jnp.max(scores, axis=-1))
    decay = jnp.exp(row_max - new_max)
    probs = jnp.exp(scores - new_max[..., None])
    row_sum = row_sum * decay + jnp.sum(probs, axis=-1)
    update = jnp.einsum(
        "hgrk,khd->hgrd",
        probs.astype(jnp.bfloat16),
        value_rows.reshape(-1, kv_heads, HD),
        preferred_element_type=jnp.float32,
    )
    weighted = weighted * decay[..., None] + update
    return (new_max, row_sum, weighted)


def finish_state(state):
    row_max, row_sum, weighted = state
    result = weighted / row_sum[..., None]
    row_count = result.shape[2]
    return jnp.transpose(result, (2, 0, 1, 3)).reshape(row_count, -1).astype(jnp.bfloat16)


def causal_step(state, query_heads, positions, key_rows, value_rows, key_positions):

    def run_block(current):
        allowed = key_positions[None, :] <= positions[:, None]
        return block_update(current, query_heads, key_rows, value_rows, allowed)

    def keep_block(current):
        return current

    return lax.cond(key_positions[0] <= positions[-1], run_block, keep_block, state)


def memory_attend(query_part, key_rows, value_rows):
    count = key_rows.shape[0]
    width = math.gcd(count, key_block)
    query_heads = split_heads(query_part)

    def memory_inner(step_no, state):
        key_part = lax.dynamic_slice_in_dim(key_rows, step_no * width, width, 0)
        value_part = lax.dynamic_slice_in_dim(value_rows, step_no * width, width, 0)
        return block_update(state, query_heads, key_part, value_part, None)

    start_state = fresh_state(query_part.shape[0], query_heads.shape[1])
    return finish_state(lax.fori_loop(0, count // width, memory_inner, start_state))


def list_memory(query_cols, got_keys, got_values, pick):
    width = got_keys.shape[-1]
    slot_total = got_keys.shape[0] * got_keys.shape[1]
    mine_keys = got_keys.reshape(slot_total, MROWS, width)[pick]
    mine_values = got_values.reshape(slot_total, MROWS, width)[pick]
    list_keys = mine_keys.reshape(TOPM * MROWS, width)
    list_values = mine_values.reshape(TOPM * MROWS, width)
    memory_parts = memory_attend(query_cols, list_keys, list_values)
    return memory_parts


def request_table(slots, owners_count, capacity, local_count):
    entries = slots.shape[0]
    owner = slots // local_count
    local = slots % local_count
    order = jnp.arange(entries, dtype=jnp.int32)
    earlier = (owner[:, None] == owner[None, :]) & (order[None, :] < order[:, None])
    rank = jnp.sum(earlier.astype(jnp.int32), axis=1)
    chosen = (owner[:, None, None] == jnp.arange(owners_count, dtype=jnp.int32)[None, :, None]) & (
        rank[:, None, None] == jnp.arange(capacity, dtype=jnp.int32)[None, None, :]
    )
    table = jnp.sum(jnp.where(chosen, local[:, None, None] + 1, 0), axis=0) - 1
    return (table, owner, rank)


def lookup_slots(wanted_ids, block_slot):
    hits = wanted_ids[..., None] == jnp.arange(block_slot.shape[0], dtype=jnp.int32)
    return jnp.sum(jnp.where(hits, block_slot, 0), axis=-1)


def on_device(
    queries, ctx_keys, ctx_values, store_keys, store_values, block_ids, block_slot, gate_logit
):
    shard_rows = queries.shape[0]
    half = shard_rows // 2
    devices = lax.axis_size("seq")
    my_index = lax.axis_index("seq")
    lists = shard_rows // QBLK
    capacity = lists * CAP
    local_count = store_keys.shape[0]
    my_slots = lookup_slots(block_ids.reshape(-1), block_slot)
    my_table, my_owner, my_rank = request_table(my_slots, devices, capacity, local_count)
    wanted = lax.all_to_all(my_table, "seq", split_axis=0, concat_axis=0, tiled=True)
    rows_wanted = jnp.maximum(wanted, 0)
    pick = my_owner * capacity + my_rank
    got_keys, got_values = (
        lax.all_to_all(store_keys[rows_wanted], "seq", split_axis=0, concat_axis=0, tiled=True),
        lax.all_to_all(store_values[rows_wanted], "seq", split_axis=0, concat_axis=0, tiled=True),
    )
    memory = list_memory(queries, got_keys, got_values, pick)
    base = my_index * shard_rows
    first_pos = base + jnp.arange(half, dtype=jnp.int32)
    first_heads = split_heads(queries[:half])
    moved = queries[half:]
    second_pos = my_index * shard_rows + half + jnp.arange(half, dtype=jnp.int32)
    second_heads = split_heads(moved)
    start_states = (fresh_state(half, KVH), fresh_state(half, KVH))
    key_piece = lax.all_gather(ctx_keys, "seq", axis=0, tiled=True)
    value_piece = lax.all_gather(ctx_values, "seq", axis=0, tiled=True)
    count = key_piece.shape[0]
    width = math.gcd(count, key_block)

    def take_inner(step_no, current):
        offset = step_no * width
        key_part = lax.dynamic_slice_in_dim(key_piece, offset, width, 0)
        value_part = lax.dynamic_slice_in_dim(value_piece, offset, width, 0)
        key_positions = offset + jnp.arange(width, dtype=jnp.int32)
        return (
            causal_step(current[0], first_heads, first_pos, key_part, value_part, key_positions),
            causal_step(current[1], second_heads, second_pos, key_part, value_part, key_positions),
        )

    states = lax.fori_loop(0, count // width, take_inner, start_states)
    first_context = finish_state(states[0])
    second_context = finish_state(states[1])
    context = jnp.concatenate([first_context, second_context], axis=0)
    gate = jnp.repeat(jax.nn.sigmoid(gate_logit), HD)
    memory_wide = lax.optimization_barrier(memory).astype(jnp.float32)
    context_wide = lax.optimization_barrier(context).astype(jnp.float32)
    return (gate * memory_wide + (1.0 - gate) * context_wide).astype(jnp.bfloat16)


def solution(mesh):
    placed = (
        P(("groups", "seq"), None),
        P(("groups", "seq"), None),
        P(("groups", "seq"), None),
        P(("groups", "seq"), None, None),
        P(("groups", "seq"), None, None),
        P(("groups", "seq"), None),
        P("groups"),
        P(),
    )
    return jax.shard_map(
        on_device, mesh=mesh, in_specs=placed, out_specs=P(("groups", "seq"), None), check_vma=False
    )
```

profile of v0, /device:TPU:31, one launch (start us, length us, event | category | flops | bytes accessed | tf_op | source)
XLA Modules:
  0.0 462.6 jit_solution(4397273095732336967)
XLA Ops:
  8.6 8.2 %all_to_all.16 = s32[16,1,2]{2,1,0:T(1,128)S(1)} all-to-all(s32[16,1,2]{2,1,0:T(1,128)S(1)} %copy.90), channel_id=1, replica_groups=mesh['groups'=2,'seq'=16] {'seq'}, dimensions={0} | all-to-all | bytes 256 | tf_op jit(solution)/shard_map/all_to_all | solution.py:136
  16.9 2.7 gather_fusion
  19.6 9.0 %all-to-all-start.1 = ((bf16[16,2,128,512]{3,2,1,0:T(8,128)(2,1)}), bf16[16,2,128,512]{3,2,1,0:T(8,128)(2,1)}, u32[]{:S(2)}, u32[]{:S(2)}) async-start(bf16[16,2,128,512]{3,2,1,0:T(8,128)(2,1)} %bitcast.133), calls=%async_computation.1 | async-start | bytes 8388608 | tf_op jit(solution)/shard_map/all_to_all | solution.py:140
  29.4 2.8 gather_fusion.2
  32.1 124.0 %all-to-all-done.1 = bf16[16,2,128,512]{3,2,1,0:T(8,128)(2,1)} async-done(((bf16[16,2,128,512]{3,2,1,0:T(8,128)(2,1)}), bf16[16,2,128,512]{3,2,1,0:T(8,128)(2,1)}, u32[]{:S(2)}, u32[]{:S(2)}) %all-to-all-start.1) | async-done | bytes 4194336 | tf_op jit(solution)/shard_map/all_to_all | solution.py:140
  156.1 5.9 %all-to-all-start.2 = ((bf16[16,2,128,512]{3,2,1,0:T(8,128)(2,1)}), bf16[16,2,128,512]{3,2,1,0:T(8,128)(2,1)}, u32[]{:S(2)}, u32[]{:S(2)}) async-start(bf16[16,2,128,512]{3,2,1,0:T(8,128)(2,1)} %bitcast.132), calls=%async_computation.2 | async-start | bytes 8388608 | tf_op jit(solution)/shard_map/all_to_all | solution.py:141
  169.6 142.3 %while.41 = (s32[]{:T(128)}, f32[4,4,128]{2,1,0:T(4,128)S(1)}, f32[4,4,128]{2,1,0:T(4,128)S(1)}, f32[4,4,128,128]{3,2,1,0:T(8,128)}, f32[4,4,128]{2,1,0:T(4,128)...) while((s32[]{:T(128)}, f32[4,4,128]{2,1,0:T(4,128)S(1)}, ...), condition=%wide.region_16.17_spmd, body=%wide.region_7.16_spmd.sunk | while | flops 2194940928 | bytes 149173872 | solution.py:166
  173.9 15.3 %conditional.5 = ((f32[4,4,128]{2,1,0:T(4,128)S(1)}, f32[4,4,128]{2,1,0:T(4,128)S(1)}, f32[4,4,128,128]{3,2,1,0:T(8,128)})) conditional(s32[]{:T(128)} %bitcast.115, (f32[4,4,128]{2,1,0:T(4,128)S(1)}, f32[4,4,128]{2,1,0:T(4,128)S(1)}, f32[4,4,128,128]{3,2,1,0:T(8,128)}) %tuple.100, (s32[1024]{0:T(1024)S(1)}, s32[128]{0:T(128)S(1)}, ...), branch_computations={%region_12.12_spmd, %region_13.15_spmd} | conditional | flops 1097469952 | bytes 68293184 | solution.py:77
  176.9 3.2 copy-done.2
  182.2 7.1 %fusion.20 = f32[4,4,128,128]{3,2,1,0:T(8,128)} fusion(f32[4,1024,128,4]{2,1,3,0:T(8,128)} %copy-done.2, f32[4,4,128]{2,1,0:T(4,128)S(1)} %max.23, pred[128,1024]{0,1:T(8,128)(4,1)S(1)} %broadcast_compare_fusion.1, bf16[1024,4,128,1]{2,1,0,3:T(4,128)(2,1)S(1)} %bitcast.128, f32[4,4,128,128]{3,2,1,0:T(8,128)} %get-tuple-element.397, ...), kind=kOutput, calls=%fused_computation.27 | convolution fusion | flops 545783808 | bytes 11681792 | tf_op jit(solution)/shard_map/while/body/eval_jaxpr/cond/branch_1_fun/hgrk,khd->hgrd/dot_general | solution.py:51
  191.1 14.2 %conditional.4 = ((f32[4,4,128]{2,1,0:T(4,128)S(1)}, f32[4,4,128]{2,1,0:T(4,128)S(1)}, f32[4,4,128,128]{3,2,1,0:T(8,128)})) conditional(s32[]{:T(128)} %bitcast.114, (f32[4,4,128]{2,1,0:T(4,128)S(1)}, f32[4,4,128]{2,1,0:T(4,128)S(1)}, f32[4,4,128,128]{3,2,1,0:T(8,128)}) %tuple.98, (s32[1024]{0:T(1024)S(1)}, s32[128]{0:T(128)S(1)}, ...), branch_computations={%region_8.8_spmd, %region_9.11_spmd} | conditional | flops 1097469952 | bytes 76681848 | solution.py:77
  194.1 3.2 copy-done.3
  199.4 4.9 %fusion.6 = f32[4,4,128,128]{3,2,1,0:T(8,128)S(1)} fusion(f32[4,1024,128,4]{2,1,3,0:T(8,128)} %copy-done.3, f32[4,4,128]{2,1,0:T(4,128)S(1)} %max.22, pred[128,1024]{0,1:T(8,128)(4,1)S(1)} %broadcast_compare_fusion, bf16[1024,4,128,1]{2,1,0,3:T(4,128)(2,1)S(1)} %bitcast.129, f32[4,4,128,128]{3,2,1,0:T(8,128)S(1)} %copy-done.5, f32[4,4,128]{2,1,0:T(4,128)S(1)} %bitcast.148), kind=kOutput, calls=%fused_computation.11 | convolution fusion | flops 545783808 | bytes 11681792 | tf_op jit(solution)/shard_map/while/body/eval_jaxpr/cond/branch_1_fun/hgrk,khd->hgrd/dot_general | solution.py:51
  209.5 15.4 %conditional.5 = ((f32[4,4,128]{2,1,0:T(4,128)S(1)}, f32[4,4,128]{2,1,0:T(4,128)S(1)}, f32[4,4,128,128]{3,2,1,0:T(8,128)})) conditional(s32[]{:T(128)} %bitcast.115, (f32[4,4,128]{2,1,0:T(4,128)S(1)}, f32[4,4,128]{2,1,0:T(4,128)S(1)}, f32[4,4,128,128]{3,2,1,0:T(8,128)}) %tuple.100, (s32[1024]{0:T(1024)S(1)}, s32[128]{0:T(128)S(1)}, ...), branch_computations={%region_12.12_spmd, %region_13.15_spmd} | conditional | flops 1097469952 | bytes 68293184 | solution.py:77
  210.0 2.4 fusion.16
  212.4 3.2 copy-done.2
  217.7 7.1 %fusion.20 = f32[4,4,128,128]{3,2,1,0:T(8,128)} fusion(f32[4,1024,128,4]{2,1,3,0:T(8,128)} %copy-done.2, f32[4,4,128]{2,1,0:T(4,128)S(1)} %max.23, pred[128,1024]{0,1:T(8,128)(4,1)S(1)} %broadcast_compare_fusion.1, bf16[1024,4,128,1]{2,1,0,3:T(4,128)(2,1)S(1)} %bitcast.128, f32[4,4,128,128]{3,2,1,0:T(8,128)} %get-tuple-element.397, ...), kind=kOutput, calls=%fused_computation.27 | convolution fusion | flops 545783808 | bytes 11681792 | tf_op jit(solution)/shard_map/while/body/eval_jaxpr/cond/branch_1_fun/hgrk,khd->hgrd/dot_general | solution.py:51
  226.7 14.2 %conditional.4 = ((f32[4,4,128]{2,1,0:T(4,128)S(1)}, f32[4,4,128]{2,1,0:T(4,128)S(1)}, f32[4,4,128,128]{3,2,1,0:T(8,128)})) conditional(s32[]{:T(128)} %bitcast.114, (f32[4,4,128]{2,1,0:T(4,128)S(1)}, f32[4,4,128]{2,1,0:T(4,128)S(1)}, f32[4,4,128,128]{3,2,1,0:T(8,128)}) %tuple.98, (s32[1024]{0:T(1024)S(1)}, s32[128]{0:T(128)S(1)}, ...), branch_computations={%region_8.8_spmd, %region_9.11_spmd} | conditional | flops 1097469952 | bytes 76681848 | solution.py:77
  229.7 3.2 copy-done.3
  234.9 4.9 %fusion.6 = f32[4,4,128,128]{3,2,1,0:T(8,128)S(1)} fusion(f32[4,1024,128,4]{2,1,3,0:T(8,128)} %copy-done.3, f32[4,4,128]{2,1,0:T(4,128)S(1)} %max.22, pred[128,1024]{0,1:T(8,128)(4,1)S(1)} %broadcast_compare_fusion, bf16[1024,4,128,1]{2,1,0,3:T(4,128)(2,1)S(1)} %bitcast.129, f32[4,4,128,128]{3,2,1,0:T(8,128)S(1)} %copy-done.5, f32[4,4,128]{2,1,0:T(4,128)S(1)} %bitcast.148), kind=kOutput, calls=%fused_computation.11 | convolution fusion | flops 545783808 | bytes 11681792 | tf_op jit(solution)/shard_map/while/body/eval_jaxpr/cond/branch_1_fun/hgrk,khd->hgrd/dot_general | solution.py:51
  245.0 15.4 %conditional.5 = ((f32[4,4,128]{2,1,0:T(4,128)S(1)}, f32[4,4,128]{2,1,0:T(4,128)S(1)}, f32[4,4,128,128]{3,2,1,0:T(8,128)})) conditional(s32[]{:T(128)} %bitcast.115, (f32[4,4,128]{2,1,0:T(4,128)S(1)}, f32[4,4,128]{2,1,0:T(4,128)S(1)}, f32[4,4,128,128]{3,2,1,0:T(8,128)}) %tuple.100, (s32[1024]{0:T(1024)S(1)}, s32[128]{0:T(128)S(1)}, ...), branch_computations={%region_12.12_spmd, %region_13.15_spmd} | conditional | flops 1097469952 | bytes 68293184 | solution.py:77
  248.0 3.2 copy-done.2
  253.2 7.1 %fusion.20 = f32[4,4,128,128]{3,2,1,0:T(8,128)} fusion(f32[4,1024,128,4]{2,1,3,0:T(8,128)} %copy-done.2, f32[4,4,128]{2,1,0:T(4,128)S(1)} %max.23, pred[128,1024]{0,1:T(8,128)(4,1)S(1)} %broadcast_compare_fusion.1, bf16[1024,4,128,1]{2,1,0,3:T(4,128)(2,1)S(1)} %bitcast.128, f32[4,4,128,128]{3,2,1,0:T(8,128)} %get-tuple-element.397, ...), kind=kOutput, calls=%fused_computation.27 | convolution fusion | flops 545783808 | bytes 11681792 | tf_op jit(solution)/shard_map/while/body/eval_jaxpr/cond/branch_1_fun/hgrk,khd->hgrd/dot_general | solution.py:51
  262.2 14.2 %conditional.4 = ((f32[4,4,128]{2,1,0:T(4,128)S(1)}, f32[4,4,128]{2,1,0:T(4,128)S(1)}, f32[4,4,128,128]{3,2,1,0:T(8,128)})) conditional(s32[]{:T(128)} %bitcast.114, (f32[4,4,128]{2,1,0:T(4,128)S(1)}, f32[4,4,128]{2,1,0:T(4,128)S(1)}, f32[4,4,128,128]{3,2,1,0:T(8,128)}) %tuple.98, (s32[1024]{0:T(1024)S(1)}, s32[128]{0:T(128)S(1)}, ...), branch_computations={%region_8.8_spmd, %region_9.11_spmd} | conditional | flops 1097469952 | bytes 76681848 | solution.py:77
  265.2 3.2 copy-done.3
  270.5 4.9 %fusion.6 = f32[4,4,128,128]{3,2,1,0:T(8,128)S(1)} fusion(f32[4,1024,128,4]{2,1,3,0:T(8,128)} %copy-done.3, f32[4,4,128]{2,1,0:T(4,128)S(1)} %max.22, pred[128,1024]{0,1:T(8,128)(4,1)S(1)} %broadcast_compare_fusion, bf16[1024,4,128,1]{2,1,0,3:T(4,128)(2,1)S(1)} %bitcast.129, f32[4,4,128,128]{3,2,1,0:T(8,128)S(1)} %copy-done.5, f32[4,4,128]{2,1,0:T(4,128)S(1)} %bitcast.148), kind=kOutput, calls=%fused_computation.11 | convolution fusion | flops 545783808 | bytes 11681792 | tf_op jit(solution)/shard_map/while/body/eval_jaxpr/cond/branch_1_fun/hgrk,khd->hgrd/dot_general | solution.py:51
  280.5 15.4 %conditional.5 = ((f32[4,4,128]{2,1,0:T(4,128)S(1)}, f32[4,4,128]{2,1,0:T(4,128)S(1)}, f32[4,4,128,128]{3,2,1,0:T(8,128)})) conditional(s32[]{:T(128)} %bitcast.115, (f32[4,4,128]{2,1,0:T(4,128)S(1)}, f32[4,4,128]{2,1,0:T(4,128)S(1)}, f32[4,4,128,128]{3,2,1,0:T(8,128)}) %tuple.100, (s32[1024]{0:T(1024)S(1)}, s32[128]{0:T(128)S(1)}, ...), branch_computations={%region_12.12_spmd, %region_13.15_spmd} | conditional | flops 1097469952 | bytes 68293184 | solution.py:77
  283.5 3.2 copy-done.2
  288.8 7.1 %fusion.20 = f32[4,4,128,128]{3,2,1,0:T(8,128)} fusion(f32[4,1024,128,4]{2,1,3,0:T(8,128)} %copy-done.2, f32[4,4,128]{2,1,0:T(4,128)S(1)} %max.23, pred[128,1024]{0,1:T(8,128)(4,1)S(1)} %broadcast_compare_fusion.1, bf16[1024,4,128,1]{2,1,0,3:T(4,128)(2,1)S(1)} %bitcast.128, f32[4,4,128,128]{3,2,1,0:T(8,128)} %get-tuple-element.397, ...), kind=kOutput, calls=%fused_computation.27 | convolution fusion | flops 545783808 | bytes 11681792 | tf_op jit(solution)/shard_map/while/body/eval_jaxpr/cond/branch_1_fun/hgrk,khd->hgrd/dot_general | solution.py:51
  297.7 14.2 %conditional.4 = ((f32[4,4,128]{2,1,0:T(4,128)S(1)}, f32[4,4,128]{2,1,0:T(4,128)S(1)}, f32[4,4,128,128]{3,2,1,0:T(8,128)})) conditional(s32[]{:T(128)} %bitcast.114, (f32[4,4,128]{2,1,0:T(4,128)S(1)}, f32[4,4,128]{2,1,0:T(4,128)S(1)}, f32[4,4,128,128]{3,2,1,0:T(8,128)}) %tuple.98, (s32[1024]{0:T(1024)S(1)}, s32[128]{0:T(128)S(1)}, ...), branch_computations={%region_8.8_spmd, %region_9.11_spmd} | conditional | flops 1097469952 | bytes 76681848 | solution.py:77
  300.7 3.2 copy-done.3
  306.0 4.9 %fusion.6 = f32[4,4,128,128]{3,2,1,0:T(8,128)S(1)} fusion(f32[4,1024,128,4]{2,1,3,0:T(8,128)} %copy-done.3, f32[4,4,128]{2,1,0:T(4,128)S(1)} %max.22, pred[128,1024]{0,1:T(8,128)(4,1)S(1)} %broadcast_compare_fusion, bf16[1024,4,128,1]{2,1,0,3:T(4,128)(2,1)S(1)} %bitcast.129, f32[4,4,128,128]{3,2,1,0:T(8,128)S(1)} %copy-done.5, f32[4,4,128]{2,1,0:T(4,128)S(1)} %bitcast.148), kind=kOutput, calls=%fused_computation.11 | convolution fusion | flops 545783808 | bytes 11681792 | tf_op jit(solution)/shard_map/while/body/eval_jaxpr/cond/branch_1_fun/hgrk,khd->hgrd/dot_general | solution.py:51
  317.8 5.0 %gather_fusion.1 = bf16[32,128,512]{2,1,0:T(8,128)(2,1)} fusion(bf16[32,128,512]{2,1,0:T(8,128)(2,1)} %bitcast.12, s32[1024]{0:T(1024)S(1)} %pad_clamp_fusion), kind=kCustom, calls=%fused_computation.1 | custom fusion | bytes 8388736 | tf_op jit(solution)/shard_map/gather | solution.py:97
  322.7 4.9 %gather_fusion.3 = bf16[32,128,512]{2,1,0:T(8,128)(2,1)} fusion(bf16[32,128,512]{2,1,0:T(8,128)(2,1)} %bitcast.19, s32[1024]{0:T(1024)S(1)} %pad_clamp_fusion), kind=kCustom, calls=%fused_computation.3 | custom fusion | bytes 8388736 | tf_op jit(solution)/shard_map/gather | solution.py:98
  327.7 119.7 %while.42 = (s32[]{:T(128)}, f32[4,4,256]{2,1,0:T(4,128)S(1)}, f32[4,4,256]{2,1,0:T(4,128)S(1)}, f32[4,4,256,128]{3,2,1,0:T(8,128)}, bf16[4096,512]{1,0:T(8,128)...) while((s32[]{:T(128)}, f32[4,4,256]{2,1,0:T(4,128)S(1)}, ...), condition=%wide.region_6.7_spmd.clone, body=%wide.region_3.6_spmd.clone.sunk | while | flops 2182631424 | bytes 66322600 | solution.py:91
  329.9 9.4 %bitcast_reduce_fusion.2 = (f32[4,4,256]{2,1,0:T(4,128)S(1)}, f32[4,1024,256,4]{2,1,3,0:T(8,128)}) fusion(bf16[1024,4,128,1]{0,2,3,1:T(8,128)(2,1)S(1)} %bitcast.127, bf16[256,4,4,128]{3,0,2,1:T(8,128)(2,1)} %get-tuple-element.841), kind=kOutput, calls=%fused_computation.40.clone.1 | convolution fusion | flops 1082126336 | bytes 18890752 | tf_op jit(solution)/shard_map/while/body/eval_jaxpr/rhgd,khd->hgrk/dot_general | solution.py:39
  339.3 8.5 %fusion.63 = f32[4,4,256]{2,1,0:T(4,128)S(1)} fusion(f32[4,1024,256,4]{2,1,3,0:T(8,128)} %get-tuple-element.747, f32[4,4,256]{2,1,0:T(4,128)S(1)} %select_maximum_fusion.2), kind=kLoop, calls=%fused_computation.43.clone.1 | loop fusion | flops 12578816 | bytes 16809984 | tf_op jit(solution)/shard_map/while/body/eval_jaxpr/reduce_sum | solution.py:50
  348.4 8.8 %fusion.65 = f32[4,4,256,128]{3,2,1,0:T(8,128)} fusion(f32[4,4,256,128]{3,2,1,0:T(8,128)} %get-tuple-element.828, bf16[1024,4,128,1]{0,2,3,1:T(8,128)(2,1)S(1)} %bitcast.124, f32[4,1024,256,4]{2,1,3,0:T(8,128)} %get-tuple-element.747, f32[4,4,256]{2,1,0:T(4,128)S(1)} %select_maximum_fusion.2, f32[4,4,256]{2,1,0:T(4,128)S(1)} %get-tuple-element.750, ...), kind=kOutput, calls=%fused_computation.48.clone.1 | convolution fusion | flops 1087897600 | bytes 22052864 | tf_op jit(solution)/shard_map/while/body/eval_jaxpr/hgrk,khd->hgrd/dot_general | solution.py:51
  359.5 9.4 %bitcast_reduce_fusion.2 = (f32[4,4,256]{2,1,0:T(4,128)S(1)}, f32[4,1024,256,4]{2,1,3,0:T(8,128)}) fusion(bf16[1024,4,128,1]{0,2,3,1:T(8,128)(2,1)S(1)} %bitcast.127, bf16[256,4,4,128]{3,0,2,1:T(8,128)(2,1)} %get-tuple-element.841), kind=kOutput, calls=%fused_computation.40.clone.1 | convolution fusion | flops 1082126336 | bytes 18890752 | tf_op jit(solution)/shard_map/while/body/eval_jaxpr/rhgd,khd->hgrk/dot_general | solution.py:39
  368.8 8.5 %fusion.63 = f32[4,4,256]{2,1,0:T(4,128)S(1)} fusion(f32[4,1024,256,4]{2,1,3,0:T(8,128)} %get-tuple-element.747, f32[4,4,256]{2,1,0:T(4,128)S(1)} %select_maximum_fusion.2), kind=kLoop, calls=%fused_computation.43.clone.1 | loop fusion | flops 12578816 | bytes 16809984 | tf_op jit(solution)/shard_map/while/body/eval_jaxpr/reduce_sum | solution.py:50
  377.9 9.3 %fusion.65 = f32[4,4,256,128]{3,2,1,0:T(8,128)} fusion(f32[4,4,256,128]{3,2,1,0:T(8,128)} %get-tuple-element.828, bf16[1024,4,128,1]{0,2,3,1:T(8,128)(2,1)S(1)} %bitcast.124, f32[4,1024,256,4]{2,1,3,0:T(8,128)} %get-tuple-element.747, f32[4,4,256]{2,1,0:T(4,128)S(1)} %select_maximum_fusion.2, f32[4,4,256]{2,1,0:T(4,128)S(1)} %get-tuple-element.750, ...), kind=kOutput, calls=%fused_computation.48.clone.1 | convolution fusion | flops 1087897600 | bytes 22052864 | tf_op jit(solution)/shard_map/while/body/eval_jaxpr/hgrk,khd->hgrd/dot_general | solution.py:51
  389.5 9.4 %bitcast_reduce_fusion.2 = (f32[4,4,256]{2,1,0:T(4,128)S(1)}, f32[4,1024,256,4]{2,1,3,0:T(8,128)}) fusion(bf16[1024,4,128,1]{0,2,3,1:T(8,128)(2,1)S(1)} %bitcast.127, bf16[256,4,4,128]{3,0,2,1:T(8,128)(2,1)} %get-tuple-element.841), kind=kOutput, calls=%fused_computation.40.clone.1 | convolution fusion | flops 1082126336 | bytes 18890752 | tf_op jit(solution)/shard_map/while/body/eval_jaxpr/rhgd,khd->hgrk/dot_general | solution.py:39
  398.9 8.5 %fusion.63 = f32[4,4,256]{2,1,0:T(4,128)S(1)} fusion(f32[4,1024,256,4]{2,1,3,0:T(8,128)} %get-tuple-element.747, f32[4,4,256]{2,1,0:T(4,128)S(1)} %select_maximum_fusion.2), kind=kLoop, calls=%fused_computation.43.clone.1 | loop fusion | flops 12578816 | bytes 16809984 | tf_op jit(solution)/shard_map/while/body/eval_jaxpr/reduce_sum | solution.py:50
  408.0 9.3 %fusion.65 = f32[4,4,256,128]{3,2,1,0:T(8,128)} fusion(f32[4,4,256,128]{3,2,1,0:T(8,128)} %get-tuple-element.828, bf16[1024,4,128,1]{0,2,3,1:T(8,128)(2,1)S(1)} %bitcast.124, f32[4,1024,256,4]{2,1,3,0:T(8,128)} %get-tuple-element.747, f32[4,4,256]{2,1,0:T(4,128)S(1)} %select_maximum_fusion.2, f32[4,4,256]{2,1,0:T(4,128)S(1)} %get-tuple-element.750, ...), kind=kOutput, calls=%fused_computation.48.clone.1 | convolution fusion | flops 1087897600 | bytes 22052864 | tf_op jit(solution)/shard_map/while/body/eval_jaxpr/hgrk,khd->hgrd/dot_general | solution.py:51
  419.6 9.4 %bitcast_reduce_fusion.2 = (f32[4,4,256]{2,1,0:T(4,128)S(1)}, f32[4,1024,256,4]{2,1,3,0:T(8,128)}) fusion(bf16[1024,4,128,1]{0,2,3,1:T(8,128)(2,1)S(1)} %bitcast.127, bf16[256,4,4,128]{3,0,2,1:T(8,128)(2,1)} %get-tuple-element.841), kind=kOutput, calls=%fused_computation.40.clone.1 | convolution fusion | flops 1082126336 | bytes 18890752 | tf_op jit(solution)/shard_map/while/body/eval_jaxpr/rhgd,khd->hgrk/dot_general | solution.py:39
  428.9 8.5 %fusion.63 = f32[4,4,256]{2,1,0:T(4,128)S(1)} fusion(f32[4,1024,256,4]{2,1,3,0:T(8,128)} %get-tuple-element.747, f32[4,4,256]{2,1,0:T(4,128)S(1)} %select_maximum_fusion.2), kind=kLoop, calls=%fused_computation.43.clone.1 | loop fusion | flops 12578816 | bytes 16809984 | tf_op jit(solution)/shard_map/while/body/eval_jaxpr/reduce_sum | solution.py:50
  438.0 9.3 %fusion.65 = f32[4,4,256,128]{3,2,1,0:T(8,128)} fusion(f32[4,4,256,128]{3,2,1,0:T(8,128)} %get-tuple-element.828, bf16[1024,4,128,1]{0,2,3,1:T(8,128)(2,1)S(1)} %bitcast.124, f32[4,1024,256,4]{2,1,3,0:T(8,128)} %get-tuple-element.747, f32[4,4,256]{2,1,0:T(4,128)S(1)} %select_maximum_fusion.2, f32[4,4,256]{2,1,0:T(4,128)S(1)} %get-tuple-element.750, ...), kind=kOutput, calls=%fused_computation.48.clone.1 | convolution fusion | flops 1087897600 | bytes 22052864 | tf_op jit(solution)/shard_map/while/body/eval_jaxpr/hgrk,khd->hgrd/dot_general | solution.py:51
  453.1 2.6 add_convert_fusion
  (193 shorter events, 88.2 us)
Async XLA Ops:
  6.5 10.3 %copy-start = (bf16[16,128,512]{2,1,0:T(8,128)(2,1)S(1)}, bf16[16,128,512]{2,1,0:T(8,128)(2,1)}, u32[]{:S(2)}) copy-start(bf16[16,128,512]{2,1,0:T(8,128)(2,1)} %param.19) | copy-start | bytes 6291460
  6.5 160.9 %all-gather.3.cloned.1.call-start = ((), (), s32[]{:S(2)}) async-start(), calls=%async_computation.3 | async-start | bytes 4456448 | tf_op jit(solution)/shard_map/all_gather | solution.py:151
  19.6 9.7 %copy-start.4 = (bf16[16,128,512]{2,1,0:T(8,128)(2,1)S(1)}, bf16[16,128,512]{2,1,0:T(8,128)(2,1)}, u32[]{:S(2)}) copy-start(bf16[16,128,512]{2,1,0:T(8,128)(2,1)} %param.20) | copy-start | bytes 6291460
  19.6 136.5 %all-to-all-start.1 = ((bf16[16,2,128,512]{3,2,1,0:T(8,128)(2,1)}), bf16[16,2,128,512]{3,2,1,0:T(8,128)(2,1)}, u32[]{:S(2)}, u32[]{:S(2)}) async-start(bf16[16,2,128,512]{3,2,1,0:T(8,128)(2,1)} %bitcast.133), calls=%async_computation.1 | async-start | bytes 8388608 | tf_op jit(solution)/shard_map/all_to_all | solution.py:140
  28.6 138.8 %all-gather.5.cloned.1.call-start = ((), (), s32[]{:S(2)}) async-start(), calls=%async_computation.4 | async-start | bytes 4456448 | tf_op jit(solution)/shard_map/all_gather | solution.py:152
  29.4 132.6 %copy-start.7 = (bf16[256,2048]{1,0:T(8,128)(2,1)S(1)}, bf16[256,2048]{1,0:T(8,128)(2,1)}, u32[]{:S(2)}) copy-start(bf16[256,2048]{1,0:T(8,128)(2,1)} %param.16) | copy-start | bytes 3145732
  156.1 9.9 %copy-start.10 = (f32[16]{0:T(128)S(1)}, f32[16]{0:T(128)}, u32[]{:S(2)}) copy-start(f32[16]{0:T(128)} %param.23) | copy-start | bytes 196
  156.1 166.6 %all-to-all-start.2 = ((bf16[16,2,128,512]{3,2,1,0:T(8,128)(2,1)}), bf16[16,2,128,512]{3,2,1,0:T(8,128)(2,1)}, u32[]{:S(2)}, u32[]{:S(2)}) async-start(bf16[16,2,128,512]{3,2,1,0:T(8,128)(2,1)} %bitcast.132), calls=%async_computation.2 | async-start | bytes 8388608 | tf_op jit(solution)/shard_map/all_to_all | solution.py:141
  176.9 3.2 copy-start.2
  194.1 3.2 copy-start.3
  194.1 5.3 %copy-start.5 = (f32[4,4,128,128]{3,2,1,0:T(8,128)S(1)}, f32[4,4,128,128]{3,2,1,0:T(8,128)}, u32[]{:S(2)}) copy-start(f32[4,4,128,128]{3,2,1,0:T(8,128)} %get-tuple-element.389) | copy-start | bytes 3145732 | tf_op jit(solution)/shard_map/while/body/eval_jaxpr/cond
  204.3 1.0 copy-start.6
  212.4 3.2 copy-start.2
  229.6 3.2 copy-start.3
  229.6 5.3 %copy-start.5 = (f32[4,4,128,128]{3,2,1,0:T(8,128)S(1)}, f32[4,4,128,128]{3,2,1,0:T(8,128)}, u32[]{:S(2)}) copy-start(f32[4,4,128,128]{3,2,1,0:T(8,128)} %get-tuple-element.389) | copy-start | bytes 3145732 | tf_op jit(solution)/shard_map/while/body/eval_jaxpr/cond
  239.9 1.0 copy-start.6
  247.9 3.2 copy-start.2
  265.2 3.2 copy-start.3
  265.2 5.3 %copy-start.5 = (f32[4,4,128,128]{3,2,1,0:T(8,128)S(1)}, f32[4,4,128,128]{3,2,1,0:T(8,128)}, u32[]{:S(2)}) copy-start(f32[4,4,128,128]{3,2,1,0:T(8,128)} %get-tuple-element.389) | copy-start | bytes 3145732 | tf_op jit(solution)/shard_map/while/body/eval_jaxpr/cond
  275.4 1.0 copy-start.6
  283.5 3.2 copy-start.2
  300.7 3.2 copy-start.3
  300.7 5.3 %copy-start.5 = (f32[4,4,128,128]{3,2,1,0:T(8,128)S(1)}, f32[4,4,128,128]{3,2,1,0:T(8,128)}, u32[]{:S(2)}) copy-start(f32[4,4,128,128]{3,2,1,0:T(8,128)} %get-tuple-element.389) | copy-start | bytes 3145732 | tf_op jit(solution)/shard_map/while/body/eval_jaxpr/cond
  310.9 1.0 copy-start.6
  327.7 125.4 %copy-start.8 = (f32[2048]{0:T(1024)S(1)}, f32[2048]{0:T(1024)}, u32[]{:S(2)}) copy-start(f32[2048]{0:T(1024)} %bitcast_subtract_fusion.1) | copy-start | bytes 24580
  327.7 125.4 %copy-start.9 = (f32[2048]{0:T(1024)S(1)}, f32[2048]{0:T(1024)}, u32[]{:S(2)}) copy-start(f32[2048]{0:T(1024)} %broadcast_bitcast_fusion) | copy-start | bytes 24580
  447.4 8.4 %copy-start.1 = (bf16[16,128,512]{2,1,0:T(8,128)(2,1)S(1)}, bf16[16,128,512]{2,1,0:T(8,128)(2,1)}, u32[]{:S(2)}) copy-start(bf16[16,128,512]{2,1,0:T(8,128)(2,1)} %param.19) | copy-start | bytes 6291460
Sparse Core Ops, SparseCore 0:
  9.5 97.7 all-gather.2
  109.4 56.4 all-gather.4
where the time goes:
time: 464 us; the launch traced here: 463 us
  matrix products  142 us (31%)
  waiting for transfers between devices  125 us (27%)
  local copies, waits for them, and re-layouts  86.5 us (19%)
  other arithmetic  60.8 us (13%)
  starting transfers between devices  14.9 us (3%)
  between operations  13.6 us (3%)
  loops' own time  11.2 us (2%)
  blocking collectives  8.18 us (2%)
    all_to_all x1, waiting for transfers between devices, on_device(): lax.all_to_all(store_keys[rows_wanted], 'seq', split_axis=0, concat_axis=...  124 us
    dot_general x12, matrix products, block_update(): jnp.einsum('hgrk,khd->hgrd', probs.astype(jnp.bfloat16), value_rows.resha...  85 us
    dot_general x12, matrix products, block_update(): jnp.einsum('rhgd,khd->hgrk', query_heads, key_rows.reshape(-1, kv_heads,...  57 us
    reduce_sum x12, other arithmetic, block_update(): row_sum = row_sum * decay + jnp.sum(probs, axis=-1)  48 us
    cond x40, local copies, waits for them, and re-layouts  29.4 us
    another operation x1, loops' own time, on_device(): states = lax.fori_loop(0, count // width, take_inner, start_states)  10.4 us
  transfers between devices with their start and end apart: 4, of which 1 were waited for; matrix products, arithmetic and copies ran while one was open for 27% of the time, Pallas kernels for 0%

commit v1 on v0

v1 whole, which is shorter than its diff:
```python
import functools

import jax
import jax.numpy as jnp
from jax import lax
from jax.experimental import pallas as pl
from jax.experimental.pallas import tpu as pltpu
from jax.sharding import PartitionSpec as P

H = 16
KVH = 4
HD = 128
GROUP = H // KVH
QBLK = 256
MROWS = 128
TOPM = 32
CAP = 2
SLAB = CAP * MROWS
TILE = 1024
SRCS = TILE // SLAB

NEG = -1e30
SCALE2 = HD ** (-0.5) * 1.4426950408889634
VMEM_LIMIT = 60 * 1024 * 1024


def request_table(slots, owners_count, capacity, local_count):
    entries = slots.shape[0]
    owner = slots // local_count
    local = slots % local_count
    order = jnp.arange(entries, dtype=jnp.int32)
    earlier = (owner[:, None] == owner[None, :]) & (order[None, :] < order[:, None])
    rank = jnp.sum(earlier.astype(jnp.int32), axis=1)
    chosen = (owner[:, None, None] == jnp.arange(owners_count, dtype=jnp.int32)[None, :, None]) & (
        rank[:, None, None] == jnp.arange(capacity, dtype=jnp.int32)[None, None, :]
    )
    return jnp.sum(jnp.where(chosen, local[:, None, None] + 1, 0), axis=0) - 1


def lookup_slots(wanted_ids, block_slot):
    hits = wanted_ids[..., None] == jnp.arange(block_slot.shape[0], dtype=jnp.int32)
    return jnp.sum(jnp.where(hits, block_slot, 0), axis=-1)


def fresh(rows):
    return (
        jnp.full((rows, 1), NEG, jnp.float32),
        jnp.zeros((rows, 1), jnp.float32),
        jnp.zeros((rows, HD), jnp.float32),
    )


def tile_update(state, q, k, v, bias=None, allowed=None):
    m, l, acc = state
    s = lax.dot_general(q, k, (((1,), (1,)), ((), ())), preferred_element_type=jnp.float32)
    s = s * SCALE2
    if bias is not None:
        s = s + bias
    if allowed is not None:
        s = jnp.where(allowed, s, NEG)
    m_new = jnp.maximum(m, jnp.max(s, axis=-1, keepdims=True))
    decay = jnp.exp2(m - m_new)
    p = jnp.exp2(s - m_new)
    l = l * decay + jnp.sum(p, axis=-1, keepdims=True)
    acc = acc * decay + jnp.dot(p.astype(jnp.bfloat16), v, preferred_element_type=jnp.float32)
    return (m_new, l, acc)


def lanes_of(j):
    return pl.ds(pl.multiple_of(j * HD, HD), HD)


def memory_kernel(size, masked, *refs):
    if masked:
        q_ref, sk_ref, sv_ref, bias_ref = refs[:4]
        refs = refs[4:]
    else:
        q_ref, sk_ref, sv_ref = refs[:3]
        bias_ref = None
        refs = refs[3:]
    (out_ref, qp, rk, rv, po, ps, ro, rs, q_sem, send_sem, recv_sem, self_sem, res_sem, st_sem) = refs
    half_size = size // 2
    me = lax.axis_index("seq")
    mine = me // half_size
    spot = me % half_size
    partner = (me + half_size) % size
    rows = q_ref.shape[0]

    barrier = pltpu.get_barrier_semaphore()

    def greet(step, carry):
        peer = mine * half_size + (spot + step) % half_size
        pl.semaphore_signal(barrier, inc=1, device_id={"seq": peer}, device_id_type=pl.DeviceIdType.MESH)
        return carry

    lax.fori_loop(1, half_size, greet, 0)
    pl.semaphore_signal(barrier, inc=1, device_id={"seq": partner}, device_id_type=pl.DeviceIdType.MESH)
    pl.semaphore_wait(barrier, half_size)

    def query_copy():
        return pltpu.make_async_remote_copy(
            src_ref=q_ref, dst_ref=qp, send_sem=q_sem.at[0], recv_sem=q_sem.at[1],
            device_id={"seq": partner}, device_id_type=pl.DeviceIdType.MESH,
        )

    def self_copies(kind):
        asker = me if kind == 0 else partner
        return (
            pltpu.make_async_copy(sk_ref.at[asker], rk.at[kind, spot], self_sem.at[kind, 0]),
            pltpu.make_async_copy(sv_ref.at[asker], rv.at[kind, spot], self_sem.at[kind, 1]),
        )

    def slab_copies(kind, step):
        peer_spot = (spot + step) % half_size
        peer = mine * half_size + peer_spot
        asker = peer if kind == 0 else (1 - mine) * half_size + peer_spot
        return tuple(
            pltpu.make_async_remote_copy(
                src_ref=src.at[asker], dst_ref=dst.at[kind, spot],
                send_sem=send_sem.at[kind, which, step], recv_sem=recv_sem.at[kind, which, spot],
                device_id={"seq": peer}, device_id_type=pl.DeviceIdType.MESH,
            )
            for which, (src, dst) in enumerate(((sk_ref, rk), (sv_ref, rv)))
        )

    def slab_arrivals(kind, step):
        from_spot = (spot + step) % half_size
        return tuple(
            pltpu.make_async_remote_copy(
                src_ref=src.at[0], dst_ref=dst.at[kind, from_spot],
                send_sem=send_sem.at[kind, which, step], recv_sem=recv_sem.at[kind, which, from_spot],
                device_id={"seq": partner}, device_id_type=pl.DeviceIdType.MESH,
            )
            for which, (src, dst) in enumerate(((sk_ref, rk), (sv_ref, rv)))
        )

    def send_all(kind):
        def send(step, carry):
            for copy in slab_copies(kind, step):
                copy.start()
            return carry

        for copy in self_copies(kind):
            copy.start()
        lax.fori_loop(1, half_size, send, 0)

    def receive_all(kind):
        def receive(step, carry):
            for copy in slab_arrivals(kind, step):
                copy.wait_recv()
            return carry

        for copy in self_copies(kind):
            copy.wait()
        lax.fori_loop(1, half_size, receive, 0)

    def result_copy(g):
        part = pl.ds(pl.multiple_of(g * GROUP * HD, GROUP * HD), GROUP * HD)
        return pltpu.make_async_remote_copy(
            src_ref=po.at[:, part], dst_ref=ro.at[:, part],
            send_sem=res_sem.at[0, g], recv_sem=res_sem.at[1, g],
            device_id={"seq": partner}, device_id_type=pl.DeviceIdType.MESH,
        )

    def stats_copy():
        return pltpu.make_async_remote_copy(
            src_ref=ps, dst_ref=rs, send_sem=st_sem.at[0], recv_sem=st_sem.at[1],
            device_id={"seq": partner}, device_id_type=pl.DeviceIdType.MESH,
        )

    def head_state(kind, source, j):
        q = source[:, lanes_of(j)]
        kv = lanes_of(j // GROUP)
        state = fresh(rows)
        for t in range(half_size // SRCS):
            k = rk[kind, t * SRCS:(t + 1) * SRCS, :, kv].reshape(TILE, HD)
            v = rv[kind, t * SRCS:(t + 1) * SRCS, :, kv].reshape(TILE, HD)
            bias = None if bias_ref is None else bias_ref[kind, :, t * TILE:(t + 1) * TILE]
            state = tile_update(state, q, k, v, bias=bias)
        return state

    lane = lax.broadcasted_iota(jnp.int32, (rows, HD), 1)

    query_copy().start()
    send_all(1)
    send_all(0)
    query_copy().wait_recv()
    receive_all(1)

    stats = jnp.zeros((rows, HD), jnp.float32)
    for g in range(KVH):

        def serve(i, st, g=g):
            j = g * GROUP + i
            m, l, acc = head_state(1, qp, j)
            po[:, lanes_of(j)] = (acc / l).astype(jnp.bfloat16)
            st = jnp.where(lane == j, m, st)
            return jnp.where(lane == j + H, l, st)

        stats = lax.fori_loop(0, GROUP, serve, stats)
        if g == KVH - 1:
            ps[...] = stats
        else:
            if g >= 1:
                result_copy(g - 1).start()
    receive_all(0)
    result_copy(KVH - 2).start()
    result_copy(KVH - 1).start()
    stats_copy().start()

    def merge(j, state):
        m, l, acc = state
        there = rs[...]
        m_far = jnp.sum(jnp.where(lane == j, there, 0.0), axis=-1, keepdims=True)
        l_far = jnp.sum(jnp.where(lane == j + H, there, 0.0), axis=-1, keepdims=True)
        top = jnp.maximum(m, m_far)
        w = jnp.exp2(m - top)
        w_far = jnp.exp2(m_far - top) * l_far
        far = ro[:, lanes_of(j)].astype(jnp.float32)
        out_ref[:, lanes_of(j)] = ((acc * w + far * w_far) / (l * w + w_far)).astype(jnp.bfloat16)

    stats_copy().wait_recv()
    for g in range(KVH):
        result_copy(g).wait_recv()

        def finish(i, carry, g=g):
            j = g * GROUP + i
            merge(j, head_state(0, q_ref, j))
            return carry

        lax.fori_loop(0, GROUP, finish, 0)

    query_copy().wait_send()
    for kind in (1, 0):

        def drain(step, carry, kind=kind):
            for copy in slab_copies(kind, step):
                copy.wait_send()
            return carry

        lax.fori_loop(1, half_size, drain, 0)
    for g in range(KVH):
        result_copy(g).wait_send()
    stats_copy().wait_send()


def memory_call(queries, send_keys, send_values, bias, size):
    rows = queries.shape[0]
    half_size = size // 2
    operands = [queries, send_keys, send_values]
    specs = [
        pl.BlockSpec(memory_space=pltpu.VMEM),
        pl.BlockSpec(memory_space=pl.ANY),
        pl.BlockSpec(memory_space=pl.ANY),
    ]
    if bias is not None:
        operands.append(bias)
        specs.append(pl.BlockSpec(memory_space=pltpu.VMEM))
    width = KVH * HD
    return pl.pallas_call(
        functools.partial(memory_kernel, size, bias is not None),
        out_shape=jax.ShapeDtypeStruct(queries.shape, jnp.bfloat16),
        in_specs=specs,
        out_specs=pl.BlockSpec(memory_space=pltpu.VMEM),
        scratch_shapes=[
            pltpu.VMEM(queries.shape, jnp.bfloat16),
            pltpu.VMEM((2, half_size, SLAB, width), jnp.bfloat16),
            pltpu.VMEM((2, half_size, SLAB, width), jnp.bfloat16),
            pltpu.VMEM(queries.shape, jnp.bfloat16),
            pltpu.VMEM((rows, HD), jnp.float32),
            pltpu.VMEM(queries.shape, jnp.bfloat16),
            pltpu.VMEM((rows, HD), jnp.float32),
            pltpu.SemaphoreType.DMA((2,)),
            pltpu.SemaphoreType.DMA((2, 2, half_size)),
            pltpu.SemaphoreType.DMA((2, 2, half_size)),
            pltpu.SemaphoreType.DMA((2, 2)),
            pltpu.SemaphoreType.DMA((2, KVH)),
            pltpu.SemaphoreType.DMA((2,)),
        ],
        compiler_params=pltpu.CompilerParams(
            collective_id=0, has_side_effects=True, vmem_limit_bytes=VMEM_LIMIT
        ),
        cost_estimate=pl.CostEstimate(
            flops=16 * 4096 * 256 * 512, bytes_accessed=200_000_000, transcendentals=16 * 4096 * 256
        ),
    )(*operands)


def context_kernel(gate_ref, pos_ref, q_ref, k_ref, v_ref, mem_ref, out_ref):
    rows = q_ref.shape[0]
    start = pos_ref[0]
    last = start // TILE
    spots = start + lax.broadcasted_iota(jnp.int32, (rows, TILE), 0)
    keys = last * TILE + lax.broadcasted_iota(jnp.int32, (rows, TILE), 1)
    allowed = keys <= spots

    def head(j, carry):
        q = q_ref[:, lanes_of(j)]
        kv = lanes_of(j // GROUP)

        def piece(t):
            at = pl.ds(pl.multiple_of(t * TILE, TILE), TILE)
            return k_ref[at, kv], v_ref[at, kv]

        k, v = piece(last)
        state = tile_update(fresh(rows), q, k, v, allowed=allowed)

        def step(t, state):
            k, v = piece(t)
            return tile_update(state, q, k, v)

        m, l, acc = lax.fori_loop(0, last, step, state)
        context = (acc / l).astype(jnp.bfloat16).astype(jnp.float32)
        memory = mem_ref[:, lanes_of(j)].astype(jnp.float32)
        g = gate_ref[j]
        out_ref[:, lanes_of(j)] = (g * memory + (1.0 - g) * context).astype(jnp.bfloat16)
        return carry

    lax.fori_loop(0, H, head, 0)


def context_call(gate, start, queries, keys, values, memory):
    full = pl.BlockSpec(memory_space=pltpu.VMEM)
    scalar = pl.BlockSpec(memory_space=pltpu.SMEM)
    return pl.pallas_call(
        context_kernel,
        out_shape=jax.ShapeDtypeStruct(queries.shape, jnp.bfloat16),
        in_specs=[scalar, scalar, full, full, full, full],
        out_specs=full,
        compiler_params=pltpu.CompilerParams(vmem_limit_bytes=VMEM_LIMIT),
    )(gate, start, queries, keys, values, memory)


def on_device(
    queries, ctx_keys, ctx_values, store_keys, store_values, block_ids, block_slot, gate_logit
):
    size = lax.axis_size("seq")
    half_size = size // 2
    me = lax.axis_index("seq")
    local_count = store_keys.shape[0]
    my_slots = lookup_slots(block_ids.reshape(-1), block_slot)
    my_table = request_table(my_slots, size, CAP, local_count)
    wanted = lax.all_to_all(my_table, "seq", split_axis=0, concat_axis=0, tiled=True)
    rows_wanted = jnp.maximum(wanted, 0)
    width = KVH * HD
    send_keys = store_keys[rows_wanted].reshape(size, SLAB, width)
    send_values = store_values[rows_wanted].reshape(size, SLAB, width)
    bias = None
    if size * CAP != TOPM:
        tables = lax.all_gather(my_table, "seq", axis=0)
        half_start = me // half_size * half_size
        two = jnp.stack([tables[me], tables[(me + half_size) % size]])
        two = lax.dynamic_slice_in_dim(two, half_start, half_size, 1).reshape(2, half_size * CAP)
        bias = jnp.repeat(jnp.where(two < 0, NEG, 0.0).astype(jnp.float32), MROWS, axis=1)[:, None, :]
    key_all = lax.all_gather(ctx_keys, "seq", axis=0, tiled=True)
    value_all = lax.all_gather(ctx_values, "seq", axis=0, tiled=True)
    memory = memory_call(queries, send_keys, send_values, bias, size)
    gate = jax.nn.sigmoid(gate_logit)
    start = jnp.reshape(me * queries.shape[0], (1,)).astype(jnp.int32)
    return context_call(gate, start, queries, key_all, value_all, memory)


def solution(mesh):
    placed = (
        P(("groups", "seq"), None),
        P(("groups", "seq"), None),
        P(("groups", "seq"), None),
        P(("groups", "seq"), None, None),
        P(("groups", "seq"), None, None),
        P(("groups", "seq"), None),
        P("groups"),
        P(),
    )
    return jax.shard_map(
        on_device, mesh=mesh, in_specs=placed, out_specs=P(("groups", "seq"), None), check_vma=False
    )
```

time: 464 us -> 291 us (0.63)
  Pallas kernels: 0 us -> 258 us
  matrix products: 142 us -> 0 us
  waiting for transfers between devices: 125 us -> 2.28 us
  local copies, waits for them, and re-layouts: 86.5 us -> 7.93 us
  other arithmetic: 60.8 us -> 2.41 us
  loops' own time: 11.2 us -> 0 us
  starting transfers between devices: 14.9 us -> 6.34 us
  blocking collectives: 8.18 us -> 0 us
    pallas_call x0 -> x2, Pallas kernels: none -> 258 us  [the longest x1 207 us: memory_call(): pl.pallas_call(functools.partial(memory_kernel, size, bias is not None),...]
    dot_general x24 -> x0, matrix products: 142 us -> none  [the longest x12 85 us: block_update(): jnp.einsum('hgrk,khd->hgrd', probs.astype(jnp.bfloat16), value_rows.resha...]
    all_to_all x2 -> x1, waiting for transfers between devices: 124 us -> 0.83 us  [on_device(): lax.all_to_all(my_table, 'seq', split_axis=0, concat_axis=0, tiled=True)]
    reduce_sum x13 -> x1, other arithmetic: 48.1 us -> 0.12 us  [request_table(): return jnp.sum(jnp.where(chosen, local[:, None, None] + 1, 0), axis=0) - 1]
    cond x40 -> x0, local copies, waits for them, and re-layouts: 29.4 us -> none
    dynamic_slice x16 -> x0, local copies, waits for them, and re-layouts: 17.7 us -> none  [the longest x8 8.87 us: memory_inner(): value_part = lax.dynamic_slice_in_dim(value_rows, step_no * width, width, 0)]
    another operation x10 -> x0, loops' own time: 11.2 us -> none  [the longest x1 10.4 us: on_device(): states = lax.fori_loop(0, count // width, take_inner, start_states)]
    all_to_all x2 -> x1, starting transfers between devices: 14.9 us -> 6.3 us  [on_device(): lax.all_to_all(my_table, 'seq', split_axis=0, concat_axis=0, tiled=True)]
  transfers between devices with their start and end apart: 4 -> 3, of which waited for: 1 -> 1; matrix products, arithmetic and copies ran while one was open for 27% -> 4% of each run, Pallas kernels for 0% -> 71%
where the time goes in v1:
time: 291 us
  Pallas kernels  258 us (89%)
  between operations  13.5 us (5%)
  local copies, waits for them, and re-layouts  7.93 us (3%)
  starting transfers between devices  6.34 us (2%)
    pallas_call x1, Pallas kernels, memory_call(): pl.pallas_call(functools.partial(memory_kernel, size, bias is not None),...  207 us
    pallas_call x1, Pallas kernels, context_call(): pl.pallas_call(context_kernel, out_shape=jax.ShapeDtypeStruct(queries.sha...  50.8 us
    all_to_all x1, starting transfers between devices, on_device(): lax.all_to_all(my_table, 'seq', split_axis=0, concat_axis=0, tiled=True)  6.3 us
  transfers between devices with their start and end apart: 3, of which 1 were waited for; matrix products, arithmetic and copies ran while one was open for 4% of the time, Pallas kernels for 71%

profile of v1, /device:TPU:31, one launch (start us, length us, event | category | flops | bytes accessed | tf_op | source)
XLA Modules:
  0.0 290.5 jit_solution(8010497633174227859)
XLA Ops:
  6.5 0.0 copy-start
  6.5 0.0 all-gather.3.cloned.1.call-start
  6.5 0.7 all-gather.3.cloned.1.call-update
  7.3 0.0 all-gather.5.cloned.1.call-start
  7.3 0.7 all-gather.5.cloned.1.call-update
  8.0 0.9 select_reduce_fusion
  8.9 0.2 convert_reduce_fusion
  9.1 0.1 select_reduce_fusion.1
  9.2 0.7 copy.12
  9.9 6.3 %all-to-all-start = ((s32[16,1,2]{2,1,0:T(1,128)}), s32[16,1,2]{2,1,0:T(1,128)S(1)}, u32[]{:S(2)}, u32[]{:S(2)}) async-start(s32[16,1,2]{2,1,0:T(1,128)} %copy.12), calls=%async_computation | async-start | bytes 16384 | tf_op jit(solution)/shard_map/all_to_all | solution.py:343
  16.2 1.2 add_divide_fusion.gate_ref
  17.4 0.8 all-to-all-done
  18.3 0.1 reshape.149
  18.4 0.0 copy-done
  18.4 2.8 gather_fusion
  21.2 4.4 %gather_fusion.1 = bf16[32,128,512]{2,1,0:T(8,128)(2,1)} fusion(bf16[16,128,512]{2,1,0:T(8,128)(2,1)} %param.12, s32[1024]{0:T(1024)S(1)} %pad_clamp_fusion), kind=kCustom, calls=%fused_computation.1 | custom fusion | bytes 8388736 | tf_op jit(solution)/shard_map/gather | solution.py:347
  25.5 207.3 %shard_map.82.mem_ref = bf16[256,2048]{1,0:T(8,128)(2,1)} custom-call(bf16[256,2048]{1,0:T(8,128)(2,1)} %q_ref.1, bf16[16,256,512]{2,1,0:T(8,128)(2,1)} %bitcast.6, bf16[16,256,512]{2,1,0:T(8,128)(2,1)} %bitcast.7), custom_call_target="tpu_custom_call" | custom-call | flops 8589934592 | bytes 200000000 | tf_op jit(solution)/shard_map/pallas_call | solution.py:260
  232.9 0.0 all-gather.3.cloned.1.call-done.k_ref
  232.9 0.0 all-gather.5.cloned.1.call-done.v_ref
  232.9 50.8 %shard_map.83 = bf16[256,2048]{1,0:T(8,128)(2,1)} custom-call(f32[16]{0:T(128)} %add_divide_fusion.gate_ref, s32[1]{0:T(128)} %bitcast.pos_ref, bf16[256,2048]{1,0:T(8,128)(2,1)} %q_ref.1, bf16[4096,512]{1,0:T(8,128)(2,1)} %all-gather.3.cloned.1.call-done.k_ref, bf16[4096,512]{1,0:T(8,128)(2,1)} %all-gather.5.cloned.1.call-done.v_ref, ...), custom_call_target="tpu_custom_call" | custom-call | tf_op jit(solution)/shard_map/pallas_call | solution.py:325
  (6 shorter events, 0.1 us)
Async XLA Ops:
  6.5 11.8 %copy-start = (bf16[16,128,512]{2,1,0:T(8,128)(2,1)S(1)}, bf16[16,128,512]{2,1,0:T(8,128)(2,1)}, u32[]{:S(2)}) copy-start(bf16[16,128,512]{2,1,0:T(8,128)(2,1)} %param.11) | copy-start | bytes 6291460
  6.5 226.3 %all-gather.3.cloned.1.call-start = ((), (), s32[]{:S(2)}) async-start(), calls=%async_computation.1 | async-start | bytes 4456448 | tf_op jit(solution)/shard_map/all_gather | solution.py:355
  7.3 225.6 %all-gather.5.cloned.1.call-start = ((), (), s32[]{:S(2)}) async-start(), calls=%async_computation.2 | async-start | bytes 4456448 | tf_op jit(solution)/shard_map/all_gather | solution.py:356
  9.9 8.3 %all-to-all-start = ((s32[16,1,2]{2,1,0:T(1,128)}), s32[16,1,2]{2,1,0:T(1,128)S(1)}, u32[]{:S(2)}, u32[]{:S(2)}) async-start(s32[16,1,2]{2,1,0:T(1,128)} %copy.12), calls=%async_computation | async-start | bytes 16384 | tf_op jit(solution)/shard_map/all_to_all | solution.py:343
Sparse Core Ops, SparseCore 0:
  9.5 87.8 all-gather.2
  99.5 70.1 all-gather.4

commit v2 on v1

--- a/solution.py
+++ b/solution.py
@@ -18,6 +18,7 @@
 SLAB = CAP * MROWS
 TILE = 1024
 SRCS = TILE // SLAB
+PLANE = 4
 
 NEG = -1e30
 SCALE2 = HD ** (-0.5) * 1.4426950408889634
@@ -70,21 +71,34 @@
     return pl.ds(pl.multiple_of(j * HD, HD), HD)
 
 
-def memory_kernel(size, masked, *refs):
+def attention_kernel(size, masked, *refs):
     if masked:
-        q_ref, sk_ref, sv_ref, bias_ref = refs[:4]
-        refs = refs[4:]
+        gate_ref, q_ref, key_ref, value_ref, sk_ref, sv_ref, bias_ref = refs[:7]
+        refs = refs[7:]
     else:
-        q_ref, sk_ref, sv_ref = refs[:3]
+        gate_ref, q_ref, key_ref, value_ref, sk_ref, sv_ref = refs[:6]
         bias_ref = None
-        refs = refs[3:]
-    (out_ref, qp, rk, rv, po, ps, ro, rs, q_sem, send_sem, recv_sem, self_sem, res_sem, st_sem) = refs
+        refs = refs[6:]
+    (out_ref, qp, rk, rv, po, ps, ro, rs, ck, cv, q_sem, send_sem, recv_sem, self_sem, res_sem, st_sem,
+     own_sem, up_sem, side_sem, core_sem) = refs
     half_size = size // 2
     me = lax.axis_index("seq")
     mine = me // half_size
     spot = me % half_size
     partner = (me + half_size) % size
     rows = q_ref.shape[0]
+    planes = size // PLANE
+    plane = me // PLANE
+    side = me % PLANE // 2
+    core = me % 2
+    above = (me + PLANE) % size
+
+    own_copies = (
+        pltpu.make_async_copy(key_ref, ck.at[me], own_sem.at[0]),
+        pltpu.make_async_copy(value_ref, cv.at[me], own_sem.at[1]),
+    )
+    for copy in own_copies:
+        copy.start()
 
     barrier = pltpu.get_barrier_semaphore()
 
@@ -95,7 +109,60 @@
 
     lax.fori_loop(1, half_size, greet, 0)
     pl.semaphore_signal(barrier, inc=1, device_id={"seq": partner}, device_id_type=pl.DeviceIdType.MESH)
-    pl.semaphore_wait(barrier, half_size)
+    for near in ((me + PLANE) % size, (me + size - PLANE) % size):
+        pl.semaphore_signal(barrier, inc=1, device_id={"seq": near}, device_id_type=pl.DeviceIdType.MESH)
+    pl.semaphore_wait(barrier, half_size + 2)
+
+    def chunk_copies(chunk, peer, send, recv):
+        return tuple(
+            pltpu.make_async_remote_copy(
+                src_ref=buf.at[chunk], dst_ref=buf.at[chunk],
+                send_sem=send(which), recv_sem=recv(which),
+                device_id={"seq": peer}, device_id_type=pl.DeviceIdType.MESH,
+            )
+            for which, buf in enumerate((ck, cv))
+        )
+
+    def up_copies(p):
+        return chunk_copies(
+            p * PLANE + me % PLANE, above, lambda w: up_sem.at[0, w, p], lambda w: up_sem.at[1, w, p]
+        )
+
+    def side_copies(p, y):
+        return chunk_copies(
+            p * PLANE + y * 2 + core, plane * PLANE + (1 - side) * 2 + core,
+            lambda w: side_sem.at[0, w, p], lambda w: side_sem.at[1, w, p],
+        )
+
+    def core_copies(p, y, c):
+        return chunk_copies(
+            p * PLANE + y * 2 + c, plane * PLANE + side * 2 + (1 - core),
+            lambda w: core_sem.at[0, w, p, y], lambda w: core_sem.at[1, w, p, y],
+        )
+
+    def start(copies):
+        for copy in copies:
+            copy.start()
+
+    def arrive(copies):
+        for copy in copies:
+            copy.wait_recv()
+
+    def left(copies):
+        for copy in copies:
+            copy.wait_send()
+
+    def pass_on(p):
+        @pl.when(plane < planes - 1)
+        def _():
+            start(up_copies(p))
+
+        start(side_copies(p, side))
+        start(core_copies(p, side, core))
+
+    def pass_side(p):
+        arrive(side_copies(p, 1 - side))
+        start(core_copies(p, 1 - side, core))
 
     def query_copy():
         return pltpu.make_async_remote_copy(
@@ -181,8 +248,20 @@
 
     lane = lax.broadcasted_iota(jnp.int32, (rows, HD), 1)
 
+    for copy in own_copies:
+        copy.wait()
+    pass_on(plane)
     query_copy().start()
     send_all(1)
+
+    def relay(t, carry):
+        arrive(up_copies(plane - t))
+        pass_on(plane - t)
+        pass_side(plane - t + 1)
+        return carry
+
+    lax.fori_loop(1, plane + 1, relay, 0)
+    pass_side(0)
     send_all(0)
     query_copy().wait_recv()
     receive_all(1)
@@ -203,10 +282,41 @@
         else:
             if g >= 1:
                 result_copy(g - 1).start()
-    receive_all(0)
     result_copy(KVH - 2).start()
+
+    def core_arrivals(t, carry):
+        arrive(core_copies(t, side, 1 - core))
+        arrive(core_copies(t, 1 - side, 1 - core))
+        return carry
+
+    lax.fori_loop(0, plane + 1, core_arrivals, 0)
     result_copy(KVH - 1).start()
     stats_copy().start()
+
+    spots = me % PLANE * rows + lax.broadcasted_iota(jnp.int32, (rows, TILE), 0)
+    allowed = lax.broadcasted_iota(jnp.int32, (rows, TILE), 1) <= spots
+
+    def context_head(j, carry):
+        q = q_ref[:, lanes_of(j)]
+        kv = lanes_of(j // GROUP)
+
+        def piece(t):
+            at = pl.ds(t * PLANE, PLANE)
+            return ck[at, :, kv].reshape(TILE, HD), cv[at, :, kv].reshape(TILE, HD)
+
+        k, v = piece(plane)
+        state = tile_update(fresh(rows), q, k, v, allowed=allowed)
+
+        def step(t, state):
+            k, v = piece(t)
+            return tile_update(state, q, k, v)
+
+        m, l, acc = lax.fori_loop(0, plane, step, state)
+        out_ref[:, lanes_of(j)] = (acc / l).astype(jnp.bfloat16)
+        return carry
+
+    lax.fori_loop(0, H, context_head, 0)
+    receive_all(0)
 
     def merge(j, state):
         m, l, acc = state
@@ -217,7 +327,10 @@
         w = jnp.exp2(m - top)
         w_far = jnp.exp2(m_far - top) * l_far
         far = ro[:, lanes_of(j)].astype(jnp.float32)
-        out_ref[:, lanes_of(j)] = ((acc * w + far * w_far) / (l * w + w_far)).astype(jnp.bfloat16)
+        memory = ((acc * w + far * w_far) / (l * w + w_far)).astype(jnp.bfloat16).astype(jnp.float32)
+        context = out_ref[:, lanes_of(j)].astype(jnp.float32)
+        gate = gate_ref[j]
+        out_ref[:, lanes_of(j)] = (gate * memory + (1.0 - gate) * context).astype(jnp.bfloat16)
 
     stats_copy().wait_recv()
     for g in range(KVH):
@@ -230,6 +343,17 @@
 
         lax.fori_loop(0, GROUP, finish, 0)
 
+    def drain_context(p, carry):
+        @pl.when(plane < planes - 1)
+        def _():
+            left(up_copies(p))
+
+        left(side_copies(p, side))
+        left(core_copies(p, side, core))
+        left(core_copies(p, 1 - side, core))
+        return carry
+
+    lax.fori_loop(0, plane + 1, drain_context, 0)
     query_copy().wait_send()
     for kind in (1, 0):
 
@@ -244,12 +368,16 @@
     stats_copy().wait_send()
 
 
-def memory_call(queries, send_keys, send_values, bias, size):
+def attention_call(gate, queries, keys, values, send_keys, send_values, bias, size):
     rows = queries.shape[0]
     half_size = size // 2
-    operands = [queries, send_keys, send_values]
+    planes = size // PLANE
+    operands = [gate, queries, keys, values, send_keys, send_values]
     specs = [
+        pl.BlockSpec(memory_space=pltpu.SMEM),
         pl.BlockSpec(memory_space=pltpu.VMEM),
+        pl.BlockSpec(memory_space=pl.ANY),
+        pl.BlockSpec(memory_space=pl.ANY),
         pl.BlockSpec(memory_space=pl.ANY),
         pl.BlockSpec(memory_space=pl.ANY),
     ]
@@ -258,7 +386,7 @@
         specs.append(pl.BlockSpec(memory_space=pltpu.VMEM))
     width = KVH * HD
     return pl.pallas_call(
-        functools.partial(memory_kernel, size, bias is not None),
+        functools.partial(attention_kernel, size, bias is not None),
         out_shape=jax.ShapeDtypeStruct(queries.shape, jnp.bfloat16),
         in_specs=specs,
         out_specs=pl.BlockSpec(memory_space=pltpu.VMEM),
@@ -270,12 +398,18 @@
             pltpu.VMEM((rows, HD), jnp.float32),
             pltpu.VMEM(queries.shape, jnp.bfloat16),
             pltpu.VMEM((rows, HD), jnp.float32),
+            pltpu.VMEM((size, rows, width), jnp.bfloat16),
+            pltpu.VMEM((size, rows, width), jnp.bfloat16),
             pltpu.SemaphoreType.DMA((2,)),
             pltpu.SemaphoreType.DMA((2, 2, half_size)),
             pltpu.SemaphoreType.DMA((2, 2, half_size)),
             pltpu.SemaphoreType.DMA((2, 2)),
             pltpu.SemaphoreType.DMA((2, KVH)),
             pltpu.SemaphoreType.DMA((2,)),
+            pltpu.SemaphoreType.DMA((2,)),
+            pltpu.SemaphoreType.DMA((2, 2, planes)),
+            pltpu.SemaphoreType.DMA((2, 2, planes)),
+            pltpu.SemaphoreType.DMA((2, 2, planes, 2)),
         ],
         compiler_params=pltpu.CompilerParams(
             collective_id=0, has_side_effects=True, vmem_limit_bytes=VMEM_LIMIT
@@ -284,51 +418,6 @@
             flops=16 * 4096 * 256 * 512, bytes_accessed=200_000_000, transcendentals=16 * 4096 * 256
         ),
     )(*operands)
-
-
-def context_kernel(gate_ref, pos_ref, q_ref, k_ref, v_ref, mem_ref, out_ref):
-    rows = q_ref.shape[0]
-    start = pos_ref[0]
-    last = start // TILE
-    spots = start + lax.broadcasted_iota(jnp.int32, (rows, TILE), 0)
-    keys = last * TILE + lax.broadcasted_iota(jnp.int32, (rows, TILE), 1)
-    allowed = keys <= spots
-
-    def head(j, carry):
-        q = q_ref[:, lanes_of(j)]
-        kv = lanes_of(j // GROUP)
-
-        def piece(t):
-            at = pl.ds(pl.multiple_of(t * TILE, TILE), TILE)
-            return k_ref[at, kv], v_ref[at, kv]
-
-        k, v = piece(last)
-        state = tile_update(fresh(rows), q, k, v, allowed=allowed)
-
-        def step(t, state):
-            k, v = piece(t)
-            return tile_update(state, q, k, v)
-
-        m, l, acc = lax.fori_loop(0, last, step, state)
-        context = (acc / l).astype(jnp.bfloat16).astype(jnp.float32)
-        memory = mem_ref[:, lanes_of(j)].astype(jnp.float32)
-        g = gate_ref[j]
-        out_ref[:, lanes_of(j)] = (g * memory + (1.0 - g) * context).astype(jnp.bfloat16)
-        return carry
-
-    lax.fori_loop(0, H, head, 0)
-
-
-def context_call(gate, start, queries, keys, values, memory):
-    full = pl.BlockSpec(memory_space=pltpu.VMEM)
-    scalar = pl.BlockSpec(memory_space=pltpu.SMEM)
-    return pl.pallas_call(
-        context_kernel,
-        out_shape=jax.ShapeDtypeStruct(queries.shape, jnp.bfloat16),
-        in_specs=[scalar, scalar, full, full, full, full],
-        out_specs=full,
-        compiler_params=pltpu.CompilerParams(vmem_limit_bytes=VMEM_LIMIT),
-    )(gate, start, queries, keys, values, memory)
 
 
 def on_device(
@@ -352,12 +441,8 @@
         two = jnp.stack([tables[me], tables[(me + half_size) % size]])
         two = lax.dynamic_slice_in_dim(two, half_start, half_size, 1).reshape(2, half_size * CAP)
         bias = jnp.repeat(jnp.where(two < 0, NEG, 0.0).astype(jnp.float32), MROWS, axis=1)[:, None, :]
-    key_all = lax.all_gather(ctx_keys, "seq", axis=0, tiled=True)
-    value_all = lax.all_gather(ctx_values, "seq", axis=0, tiled=True)
-    memory = memory_call(queries, send_keys, send_values, bias, size)
     gate = jax.nn.sigmoid(gate_logit)
-    start = jnp.reshape(me * queries.shape[0], (1,)).astype(jnp.int32)
-    return context_call(gate, start, queries, key_all, value_all, memory)
+    return attention_call(gate, queries, ctx_keys, ctx_values, send_keys, send_values, bias, size)
 
 
 def solution(mesh):

time: 291 us -> 282 us (0.969)
  the two profiles are of different devices: /device:TPU:31 before, /device:TPU:8 now
where the time goes in v2:
time: 282 us
  Pallas kernels  259 us (92%)
  local copies, waits for them, and re-layouts  10.2 us (4%)
  starting transfers between devices  6.3 us (2%)
  waiting for transfers between devices  3.71 us (1%)
    pallas_call x1, Pallas kernels, attention_call(): pl.pallas_call(functools.partial(attention_kernel, size, bias is not None...  259 us
    all_to_all x1, starting transfers between devices, on_device(): lax.all_to_all(my_table, 'seq', split_axis=0, concat_axis=0, tiled=True)  6.3 us
  transfers between devices with their start and end apart: 1, of which 1 were waited for; matrix products, arithmetic and copies ran while one was open for 0% of the time, Pallas kernels for 0%

profile of v2, /device:TPU:8, one launch (start us, length us, event | category | flops | bytes accessed | tf_op | source)
XLA Modules:
  0.0 281.9 jit_solution(1105096014569082240)
XLA Ops:
  0.0 0.0 copy-start
  0.0 1.0 select_reduce_fusion
  1.0 0.2 convert_reduce_fusion
  1.2 0.1 select_reduce_fusion.1
  1.4 0.7 copy.12
  2.0 6.3 %all-to-all-start = ((s32[16,1,2]{2,1,0:T(1,128)}), s32[16,1,2]{2,1,0:T(1,128)S(1)}, u32[]{:S(2)}, u32[]{:S(2)}) async-start(s32[16,1,2]{2,1,0:T(1,128)} %copy.12), calls=%async_computation | async-start | bytes 16384 | tf_op jit(solution)/shard_map/all_to_all | solution.py:432
  8.3 1.2 add_divide_fusion.refs_0_
  9.6 3.7 %all-to-all-done = s32[16,1,2]{2,1,0:T(1,128)S(1)} async-done(((s32[16,1,2]{2,1,0:T(1,128)}), s32[16,1,2]{2,1,0:T(1,128)S(1)}, u32[]{:S(2)}, u32[]{:S(2)}) %all-to-all-start) | async-done | bytes 160 | tf_op jit(solution)/shard_map/all_to_all | solution.py:432
  13.3 0.1 reshape.145
  13.4 0.0 copy-done
  13.4 2.8 gather_fusion.1
  16.2 4.3 %gather_fusion = bf16[32,128,512]{2,1,0:T(8,128)(2,1)} fusion(bf16[16,128,512]{2,1,0:T(8,128)(2,1)} %param.11, s32[1024]{0:T(1024)S(1)} %pad_clamp_fusion), kind=kCustom, calls=%fused_computation | custom fusion | bytes 8388736 | tf_op jit(solution)/shard_map/gather | solution.py:435
  20.5 259.0 %shard_map.82 = bf16[256,2048]{1,0:T(8,128)(2,1)} custom-call(f32[16]{0:T(128)} %add_divide_fusion.refs_0_, bf16[256,2048]{1,0:T(8,128)(2,1)} %refs_1_.1, bf16[256,512]{1,0:T(8,128)(2,1)} %refs_2_.1, bf16[256,512]{1,0:T(8,128)(2,1)} %refs_3_.1, bf16[16,256,512]{2,1,0:T(8,128)(2,1)} %bitcast.6, bf16[16,256,512]{2,1,0:T(8,128)(2,1)} %bitcast.5), custom_call_target="tpu_custom_call" | custom-call | flops 8589934592 | bytes 200000000 | tf_op jit(solution)/shard_map/pallas_call | solution.py:388
  279.6 2.3 copy.14
  (6 shorter events, 0.1 us)
Async XLA Ops:
  0.0 13.4 %copy-start = (bf16[16,128,512]{2,1,0:T(8,128)(2,1)S(1)}, bf16[16,128,512]{2,1,0:T(8,128)(2,1)}, u32[]{:S(2)}) copy-start(bf16[16,128,512]{2,1,0:T(8,128)(2,1)} %param.12) | copy-start | bytes 6291460
  2.0 11.2 %all-to-all-start = ((s32[16,1,2]{2,1,0:T(1,128)}), s32[16,1,2]{2,1,0:T(1,128)S(1)}, u32[]{:S(2)}, u32[]{:S(2)}) async-start(s32[16,1,2]{2,1,0:T(1,128)} %copy.12), calls=%async_computation | async-start | bytes 16384 | tf_op jit(solution)/shard_map/all_to_all | solution.py:432

commit v3 on v2

--- a/solution.py
+++ b/solution.py
@@ -251,8 +251,6 @@
     for copy in own_copies:
         copy.wait()
     pass_on(plane)
-    query_copy().start()
-    send_all(1)
 
     def relay(t, carry):
         arrive(up_copies(plane - t))
@@ -260,8 +258,12 @@
         pass_side(plane - t + 1)
         return carry
 
-    lax.fori_loop(1, plane + 1, relay, 0)
-    pass_side(0)
+    @pl.when(plane >= 1)
+    def _():
+        relay(1, 0)
+
+    query_copy().start()
+    send_all(1)
     send_all(0)
     query_copy().wait_recv()
     receive_all(1)
@@ -282,6 +284,14 @@
         else:
             if g >= 1:
                 result_copy(g - 1).start()
+            if g == 1:
+
+                @pl.when(plane >= 2)
+                def _():
+                    relay(2, 0)
+
+    lax.fori_loop(3, plane + 1, relay, 0)
+    pass_side(0)
     result_copy(KVH - 2).start()
 
     def core_arrivals(t, carry):

time: 282 us -> 282 us (level)
  the two profiles are of different devices: /device:TPU:8 before, /device:TPU:31 now
where the time goes in v3:
time: 282 us; the launch traced here: 280 us
  Pallas kernels  260 us (92%)
  local copies, waits for them, and re-layouts  10.2 us (4%)
  starting transfers between devices  6.3 us (2%)
    pallas_call x1, Pallas kernels, attention_call(): pl.pallas_call(functools.partial(attention_kernel, size, bias is not None...  260 us
    all_to_all x1, starting transfers between devices, on_device(): lax.all_to_all(my_table, 'seq', split_axis=0, concat_axis=0, tiled=True)  6.3 us
  transfers between devices with their start and end apart: 1, of which 1 were waited for; matrix products, arithmetic and copies ran while one was open for 0% of the time, Pallas kernels for 0%

profile of v3, /device:TPU:31, one launch (start us, length us, event | category | flops | bytes accessed | tf_op | source)
XLA Modules:
  0.0 280.1 jit_solution(2413930918507222627)
XLA Ops:
  0.0 0.0 copy-start
  0.0 1.0 select_reduce_fusion
  1.0 0.2 convert_reduce_fusion
  1.2 0.1 select_reduce_fusion.1
  1.4 0.7 copy.12
  2.0 6.3 %all-to-all-start = ((s32[16,1,2]{2,1,0:T(1,128)}), s32[16,1,2]{2,1,0:T(1,128)S(1)}, u32[]{:S(2)}, u32[]{:S(2)}) async-start(s32[16,1,2]{2,1,0:T(1,128)} %copy.12), calls=%async_computation | async-start | bytes 16384 | tf_op jit(solution)/shard_map/all_to_all | solution.py:442
  8.3 1.2 add_divide_fusion.refs_0_
  9.6 0.8 all-to-all-done
  10.4 0.1 reshape.145
  10.5 0.0 copy-done
  10.5 2.8 gather_fusion.1
  13.3 4.3 %gather_fusion = bf16[32,128,512]{2,1,0:T(8,128)(2,1)} fusion(bf16[16,128,512]{2,1,0:T(8,128)(2,1)} %param.11, s32[1024]{0:T(1024)S(1)} %pad_clamp_fusion), kind=kCustom, calls=%fused_computation | custom fusion | bytes 8388736 | tf_op jit(solution)/shard_map/gather | solution.py:445
  17.6 260.1 %shard_map.82 = bf16[256,2048]{1,0:T(8,128)(2,1)} custom-call(f32[16]{0:T(128)} %add_divide_fusion.refs_0_, bf16[256,2048]{1,0:T(8,128)(2,1)} %refs_1_.1, bf16[256,512]{1,0:T(8,128)(2,1)} %refs_2_.1, bf16[256,512]{1,0:T(8,128)(2,1)} %refs_3_.1, bf16[16,256,512]{2,1,0:T(8,128)(2,1)} %bitcast.6, bf16[16,256,512]{2,1,0:T(8,128)(2,1)} %bitcast.5), custom_call_target="tpu_custom_call" | custom-call | flops 8589934592 | bytes 200000000 | tf_op jit(solution)/shard_map/pallas_call | solution.py:398
  277.8 2.3 copy.14
  (6 shorter events, 0.1 us)
Async XLA Ops:
  0.0 10.5 %copy-start = (bf16[16,128,512]{2,1,0:T(8,128)(2,1)S(1)}, bf16[16,128,512]{2,1,0:T(8,128)(2,1)}, u32[]{:S(2)}) copy-start(bf16[16,128,512]{2,1,0:T(8,128)(2,1)} %param.12) | copy-start | bytes 6291460
  2.0 8.3 %all-to-all-start = ((s32[16,1,2]{2,1,0:T(1,128)}), s32[16,1,2]{2,1,0:T(1,128)S(1)}, u32[]{:S(2)}, u32[]{:S(2)}) async-start(s32[16,1,2]{2,1,0:T(1,128)} %copy.12), calls=%async_computation | async-start | bytes 16384 | tf_op jit(solution)/shard_map/all_to_all | solution.py:442
